TPU v7x, 32 devices: a whole 2x2x4 slice. The times are simulated.
32 devices in a mesh: parts: 2 (over y), seq: 4 (over z), chan: 4 (over x, core).
Axes of the slice: x: 2, y: 2, z: 4, core: 2. Of those that a mesh axis runs over, the one named last changes fastest.
Arguments:
- records: bfloat16 [8, 1536, 512], P('parts', 'seq', 'chan'), parts along dimension 0, may hold values from -6 to 6
- norm_gain: float32 [512], replicated, may hold values from 0.1 to 1.9
- in_projection: bfloat16 [512, 3, 512], P(None, None, 'chan'), may hold values from -0.25 to 0.25
- short_kernel: float32 [3, 3, 512], P(None, None, 'chan'), may hold values from -3.5 to 3.5
- long_filter: bfloat16 [16, 1536], P('chan', 'seq'), may hold values from -1.6 to 1.6
- skip_gain: float32 [512], P('chan'), may hold values from 0.5 to 1.5
- out_projection: bfloat16 [512, 512], P('chan'), may hold values from -0.25 to 0.25
Outputs:
- mixed: bfloat16 [8, 1536, 512], P('parts', 'seq', 'chan'), parts along dimension 0
There are 2 independent parts, one for each index of `parts`. A program takes and returns all parts, laid end to end along the dimension named above; an argument that names none is the same for every part. Nothing has to cross between parts.
All inputs are finite; a program needn't handle non-finite values.
Results may differ from a plain program's by a relative error of at most 0.015.
Values may be sent and summed in bfloat16 or wider, within the bound.
A program may use at most 128 MiB of HBM per device.

v0:
```python
import jax
import jax.numpy as jnp
from jax import lax
from jax.sharding import PartitionSpec as P


def from_behind(block, axis, distance):
    devices = range(lax.axis_size(axis))
    route = [(i - distance, i) for i in devices if i - distance in devices]
    return lax.ppermute(block, axis, route)


def block_terms(taps_padded, offset, block_source, block_len):
    filter_count = taps_padded.shape[0]
    window = lax.dynamic_slice_in_dim(taps_padded, offset + 1, 2 * block_len - 1, 1)
    flipped = window[:, ::-1]
    padded = jnp.pad(flipped, ((0, 0), (0, 1)))
    tiled_taps = jnp.tile(padded, (1, block_len))
    toeplitz = tiled_taps[:, block_len - 1 : block_len - 1 + block_len * (2 * block_len - 1)]
    toeplitz = toeplitz.reshape(filter_count, block_len, 2 * block_len - 1)[:, :, :block_len]
    record_count = block_source.shape[0]
    grouped = block_source.reshape(record_count, block_len, filter_count, -1)
    return jnp.einsum("fab,rbfg->rafg", toeplitz, grouped, preferred_element_type=jnp.float32)


def body(records, norm_gain, in_projection, short_kernel, long_filter, skip_gain, out_projection):
    gathered = lax.all_gather(records, "chan", axis=2, tiled=True)
    widened = gathered.astype(jnp.float32)
    inv_rms = lax.rsqrt(jnp.mean(widened * widened, axis=-1, keepdims=True) + 1e-06)
    normed = (widened * inv_rms * norm_gain).astype(jnp.bfloat16)
    projected = jnp.einsum(
        "rtd,dkc->rtkc", normed, in_projection, preferred_element_type=jnp.float32
    ).astype(jnp.bfloat16)
    rim_rows = from_behind(projected[:, -2:], "seq", 1)
    extended = jnp.concatenate([rim_rows, projected], axis=1).astype(jnp.float32)
    streams = (
        short_kernel[0] * extended[:, 2:]
        + short_kernel[1] * extended[:, 1:-1]
        + short_kernel[2] * extended[:, :-2]
    )
    query_gate = streams[:, :, 0]
    gated_source = (streams[:, :, 1] * streams[:, :, 2]).astype(jnp.bfloat16)
    record_count = gated_source.shape[0]
    block_len = gated_source.shape[1]
    channels = gated_source.shape[2]
    all_taps = lax.all_gather(long_filter, "seq", axis=1, tiled=True)
    taps_padded = jnp.concatenate(
        [jnp.zeros((all_taps.shape[0], block_len), jnp.bfloat16), all_taps], axis=1
    )
    my_start = lax.axis_index("seq") * block_len
    cycle_stops = lax.axis_size("seq")
    long_sum = block_terms(taps_padded, 0, gated_source, block_len)

    def advance(stop_index, state):
        running_sum, visiting = state
        visiting = from_behind(visiting, "seq", 1)
        lag_start = stop_index * block_len
        running_sum = lax.cond(
            lag_start <= my_start,
            lambda running: running + block_terms(taps_padded, lag_start, visiting, block_len),
            lambda running: running,
            running_sum,
        )
        return (running_sum, visiting)

    long_sum, visiting = lax.fori_loop(1, cycle_stops, advance, (long_sum, gated_source))
    long_out = long_sum.reshape(
        record_count, block_len, channels
    ) + skip_gain * gated_source.astype(jnp.float32)
    gated = (query_gate * long_out).astype(jnp.bfloat16)
    partial_terms = jnp.einsum(
        "rtc,cd->rtd", gated, out_projection, preferred_element_type=jnp.float32
    )
    return lax.psum_scatter(
        partial_terms.astype(jnp.bfloat16), "chan", scatter_dimension=2, tiled=True
    )


def solution(mesh):
    placed = (
        P("parts", "seq", "chan"),
        P(),
        P(None, None, "chan"),
        P(None, None, "chan"),
        P("chan", "seq"),
        P("chan"),
        P("chan", None),
    )
    return jax.shard_map(
        body, mesh=mesh, in_specs=placed, out_specs=P("parts", "seq", "chan"), check_vma=False
    )
```

profile of v0, /device:TPU:29, one launch (start us, length us, event | category | flops | bytes accessed | tf_op | source)
XLA Modules:
  0.0 200.5 jit_solution(438159001702864460)
XLA Ops:
  6.5 0.7 all-gather.2.cloned.1.call-update
  7.3 10.2 %all_gather.7 = bf16[4,1536]{1,0:T(4,128)(2,1)S(1)} all-gather(bf16[4,384]{1,0:T(4,128)(2,1)} %param.15), channel_id=1, replica_groups=mesh['parts'=2,'seq'=4,'chan'=4] {'seq'}, dimensions={1}, use_global_device_ids=true | all-gather | bytes 15360 | tf_op jit(solution)/shard_map/all_gather | solution.py:46
  17.6 0.5 reverse.1
  18.2 0.2 broadcast_bitcast_fusion.1
  18.4 11.8 %all-gather.2.cloned.1.call-done = bf16[4,384,512]{2,1,0:T(8,128)(2,1)} async-done(((bf16[4,384,128]{2,1,0:T(8,128)(2,1)}), bf16[4,384,512]{2,1,0:T(8,128)(2,1)}) %all-gather.2.cloned.1.call-update) | async-done | bytes 1572880 | tf_op jit(solution)/shard_map/all_gather | solution.py:27
  30.1 1.8 fusion.2
  32.0 2.4 %fusion.12 = bf16[4,384,3,128]{3,1,2,0:T(8,128)(2,1)S(1)} fusion(bf16[4,384,512]{2,1,0:T(8,128)(2,1)} %all-gather.2.cloned.1.call-done, f32[512]{0:T(512)S(1)} %copy-done.9, f32[4,384]{1,0:T(4,128)S(1)} %add_rsqrt_fusion, bf16[512,3,128]{2,0,1:T(8,128)(2,1)S(1)} %copy-done), kind=kOutput, calls=%fused_computation.19 | convolution fusion | flops 607715328 | bytes 3153920 | tf_op jit(solution)/shard_map/rtd,dkc->rtkc/dot_general | solution.py:31
  34.5 1.3 collective-permute-start.1
  35.8 1.8 copy.32
  37.6 2.8 %slice.63 = bf16[4,294528]{1,0:T(4,128)(2,1)} slice(bf16[4,294912]{1,0:T(4,128)(2,1)S(1)} %bitcast.67), slice={[0:4], [383:294911]} | slice | bytes 4712448 | tf_op jit(solution)/shard_map/slice | solution.py:19
  40.4 3.3 %reshape.52 = bf16[1178112]{0:T(1024)(128)(2,1)S(1)} reshape(bf16[4,294528]{1,0:T(4,128)(2,1)} %slice.63) | data formatting | bytes 4712448
  43.7 6.5 %reshape.40 = bf16[4,384,767]{2,1,0:T(8,128)(2,1)} reshape(bf16[1178112]{0:T(1024)(128)(2,1)S(1)} %reshape.52) | data formatting | bytes 4712448 | tf_op jit(solution)/shard_map/reshape | solution.py:20
  50.2 1.5 maximum_convert_fusion
  51.7 0.7 fusion.5
  52.5 1.3 copy-done.1
  53.9 0.8 fusion.25
  54.7 0.2 copy.21
  54.9 1.9 copy.23
  56.8 1.4 convolution_bitcast_fusion
  58.3 95.5 %while.18 = (s32[]{:T(128)}, f32[4,384,4,32]{1,3,0,2:T(8,128)}, bf16[4,384,128]{1,2,0:T(8,128)(2,1)}, s32[]{:T(128)}, bf16[4,1920]{1,0:T(4,128)(2,1)S(1)}, /*index=5*/s32[]{:T(128)}, s32[]{:T(128)}) while((s32[]{:T(128)}, f32[4,384,4,32]{1,3,0,2:T(8,128)}, bf16[4,384,128]{1,2,0:T(8,128)(2,1)}, s32[]{:T(128)}, bf16[4,1920]{1,0:T(4,128)(2,1)S(1)}, ...), condition=%wide.region_4.5_spmd, body=%wide.region_1.4_spmd.sunk | while | flops 151191552 | bytes 29135044 | solution.py:66
  58.3 1.3 collective-permute-start
  59.6 11.9 %collective-permute-done = bf16[4,384,128]{1,2,0:T(8,128)(2,1)S(1)} collective-permute-done((bf16[4,384,128]{1,2,0:T(8,128)(2,1)}, bf16[4,384,128]{1,2,0:T(8,128)(2,1)S(1)}, u32[]{:S(2)}, u32[]{:S(2)}) %collective-permute-start) | collective-permute-done | bytes 393248 | tf_op jit(solution)/shard_map/while/body/eval_jaxpr/ppermute | solution.py:10
  71.4 19.2 %conditional.2 = (f32[4,384,4,32]{1,3,0,2:T(8,128)}) conditional(s32[]{:T(128)} %convert_element_type.81, f32[4,384,4,32]{1,3,0,2:T(8,128)} %get-tuple-element.182, (s32[]{:T(128)}, bf16[4,1920]{1,0:T(4,128)(2,1)S(1)}, bf16[4,384,128]{1,2,0:T(8,128)(2,1)S(1)}, f32[4,384,4,32]{1,3,0,2:T(8,128)}) %tuple.43), branch_computations={%region_2.2_spmd, %region_3.3_spmd} | conditional | flops 151191552 | bytes 26775572 | solution.py:58
  71.5 0.5 reverse
  72.2 0.2 broadcast_bitcast_fusion
  72.3 1.8 copy.31
  74.2 2.8 %slice.54 = bf16[4,294528]{1,0:T(4,128)(2,1)} slice(bf16[4,294912]{1,0:T(4,128)(2,1)S(1)} %bitcast.63), slice={[0:4], [383:294911]} | slice | bytes 4712448 | tf_op jit(solution)/shard_map/while/body/eval_jaxpr/cond/branch_1_fun/slice | solution.py:19
  76.9 3.3 %reshape.50 = bf16[1178112]{0:T(1024)(128)(2,1)S(1)} reshape(bf16[4,294528]{1,0:T(4,128)(2,1)} %slice.54) | data formatting | bytes 4712448 | tf_op jit(solution)/shard_map/while/body/eval_jaxpr/cond
  80.2 6.5 %reshape.36 = bf16[4,384,767]{2,1,0:T(8,128)(2,1)} reshape(bf16[1178112]{0:T(1024)(128)(2,1)S(1)} %reshape.50) | data formatting | bytes 4712448 | tf_op jit(solution)/shard_map/while/body/eval_jaxpr/cond/branch_1_fun/reshape | solution.py:20
  86.8 1.8 fusion
  88.5 2.1 %add.44 = f32[4,384,4,32]{1,3,0,2:T(8,128)} add(f32[4,384,4,32]{1,3,0,2:T(8,128)} %get-tuple-element.108, f32[4,384,4,32]{1,3,0,2:T(8,128)S(1)} %bitcast.64) | non-fusion elementwise | flops 196608 | bytes 2359296 | tf_op jit(solution)/shard_map/while/body/eval_jaxpr/cond/branch_1_fun/add | solution.py:60
  90.7 0.8 copy.46
  91.4 1.3 collective-permute-start
  92.7 10.3 %collective-permute-done = bf16[4,384,128]{1,2,0:T(8,128)(2,1)S(1)} collective-permute-done((bf16[4,384,128]{1,2,0:T(8,128)(2,1)}, bf16[4,384,128]{1,2,0:T(8,128)(2,1)S(1)}, u32[]{:S(2)}, u32[]{:S(2)}) %collective-permute-start) | collective-permute-done | bytes 393248 | tf_op jit(solution)/shard_map/while/body/eval_jaxpr/ppermute | solution.py:10
  103.1 19.2 %conditional.2 = (f32[4,384,4,32]{1,3,0,2:T(8,128)}) conditional(s32[]{:T(128)} %convert_element_type.81, f32[4,384,4,32]{1,3,0,2:T(8,128)} %get-tuple-element.182, (s32[]{:T(128)}, bf16[4,1920]{1,0:T(4,128)(2,1)S(1)}, bf16[4,384,128]{1,2,0:T(8,128)(2,1)S(1)}, f32[4,384,4,32]{1,3,0,2:T(8,128)}) %tuple.43), branch_computations={%region_2.2_spmd, %region_3.3_spmd} | conditional | flops 151191552 | bytes 26775572 | solution.py:58
  103.1 0.5 reverse
  103.8 0.2 broadcast_bitcast_fusion
  103.9 1.8 copy.31
  105.8 2.8 %slice.54 = bf16[4,294528]{1,0:T(4,128)(2,1)} slice(bf16[4,294912]{1,0:T(4,128)(2,1)S(1)} %bitcast.63), slice={[0:4], [383:294911]} | slice | bytes 4712448 | tf_op jit(solution)/shard_map/while/body/eval_jaxpr/cond/branch_1_fun/slice | solution.py:19
  108.5 3.3 %reshape.50 = bf16[1178112]{0:T(1024)(128)(2,1)S(1)} reshape(bf16[4,294528]{1,0:T(4,128)(2,1)} %slice.54) | data formatting | bytes 4712448 | tf_op jit(solution)/shard_map/while/body/eval_jaxpr/cond
  111.8 6.5 %reshape.36 = bf16[4,384,767]{2,1,0:T(8,128)(2,1)} reshape(bf16[1178112]{0:T(1024)(128)(2,1)S(1)} %reshape.50) | data formatting | bytes 4712448 | tf_op jit(solution)/shard_map/while/body/eval_jaxpr/cond/branch_1_fun/reshape | solution.py:20
  118.4 1.8 fusion
  120.2 2.1 %add.44 = f32[4,384,4,32]{1,3,0,2:T(8,128)} add(f32[4,384,4,32]{1,3,0,2:T(8,128)} %get-tuple-element.108, f32[4,384,4,32]{1,3,0,2:T(8,128)S(1)} %bitcast.64) | non-fusion elementwise | flops 196608 | bytes 2359296 | tf_op jit(solution)/shard_map/while/body/eval_jaxpr/cond/branch_1_fun/add | solution.py:60
  122.3 0.8 copy.46
  123.0 1.3 collective-permute-start
  124.3 9.4 %collective-permute-done = bf16[4,384,128]{1,2,0:T(8,128)(2,1)S(1)} collective-permute-done((bf16[4,384,128]{1,2,0:T(8,128)(2,1)}, bf16[4,384,128]{1,2,0:T(8,128)(2,1)S(1)}, u32[]{:S(2)}, u32[]{:S(2)}) %collective-permute-start) | collective-permute-done | bytes 393248 | tf_op jit(solution)/shard_map/while/body/eval_jaxpr/ppermute | solution.py:10
  133.8 19.2 %conditional.2 = (f32[4,384,4,32]{1,3,0,2:T(8,128)}) conditional(s32[]{:T(128)} %convert_element_type.81, f32[4,384,4,32]{1,3,0,2:T(8,128)} %get-tuple-element.182, (s32[]{:T(128)}, bf16[4,1920]{1,0:T(4,128)(2,1)S(1)}, bf16[4,384,128]{1,2,0:T(8,128)(2,1)S(1)}, f32[4,384,4,32]{1,3,0,2:T(8,128)}) %tuple.43), branch_computations={%region_2.2_spmd, %region_3.3_spmd} | conditional | flops 151191552 | bytes 26775572 | solution.py:58
  133.8 0.5 reverse
  134.5 0.2 broadcast_bitcast_fusion
  134.6 1.8 copy.31
  136.5 2.8 %slice.54 = bf16[4,294528]{1,0:T(4,128)(2,1)} slice(bf16[4,294912]{1,0:T(4,128)(2,1)S(1)} %bitcast.63), slice={[0:4], [383:294911]} | slice | bytes 4712448 | tf_op jit(solution)/shard_map/while/body/eval_jaxpr/cond/branch_1_fun/slice | solution.py:19
  139.2 3.3 %reshape.50 = bf16[1178112]{0:T(1024)(128)(2,1)S(1)} reshape(bf16[4,294528]{1,0:T(4,128)(2,1)} %slice.54) | data formatting | bytes 4712448 | tf_op jit(solution)/shard_map/while/body/eval_jaxpr/cond
  142.5 6.5 %reshape.36 = bf16[4,384,767]{2,1,0:T(8,128)(2,1)} reshape(bf16[1178112]{0:T(1024)(128)(2,1)S(1)} %reshape.50) | data formatting | bytes 4712448 | tf_op jit(solution)/shard_map/while/body/eval_jaxpr/cond/branch_1_fun/reshape | solution.py:20
  149.1 1.8 fusion
  150.8 2.1 %add.44 = f32[4,384,4,32]{1,3,0,2:T(8,128)} add(f32[4,384,4,32]{1,3,0,2:T(8,128)} %get-tuple-element.108, f32[4,384,4,32]{1,3,0,2:T(8,128)S(1)} %bitcast.64) | non-fusion elementwise | flops 196608 | bytes 2359296 | tf_op jit(solution)/shard_map/while/body/eval_jaxpr/cond/branch_1_fun/add | solution.py:60
  153.0 0.8 copy.46
  153.8 1.2 copy.24
  155.0 1.2 copy.25
  156.2 1.9 convolution_convert_fusion
  158.1 1.4 copy.28
  159.6 1.4 copy.33
  161.0 30.6 %reduce-scatter.4.cloned.1.call-done = bf16[128,1536]{1,0:T(8,128)(2,1)} async-done(((bf16[512,1536]{1,0:T(8,128)(2,1)}), bf16[128,1536]{1,0:T(8,128)(2,1)}) %reduce-scatter.4.cloned.1.call-update) | async-done | bytes 393232
  191.6 1.1 reshape.49
  192.7 1.0 copy.29
  (43 shorter events, 1.0 us)
Async XLA Ops:
  6.5 25.4 %copy-start = (bf16[512,3,128]{2,0,1:T(8,128)(2,1)S(1)}, bf16[512,3,128]{2,0,1:T(8,128)(2,1)}, u32[]{:S(2)}) copy-start(bf16[512,3,128]{2,0,1:T(8,128)(2,1)} %param.13) | copy-start | bytes 1179652
  6.5 25.4 %copy-start.9 = (f32[512]{0:T(512)S(1)}, f32[512]{0:T(512)}, u32[]{:S(2)}) copy-start(f32[512]{0:T(512)} %param.12) | copy-start | bytes 6148
  6.5 23.6 %all-gather.2.cloned.1.call-start = ((), (), s32[]{:S(2)}) async-start(), calls=%async_computation.1 | async-start | bytes 1966080 | tf_op jit(solution)/shard_map/all_gather | solution.py:27
  7.3 184.3 %reduce-scatter.4.cloned.1.call-start = ((), (), s32[]{:S(2)}) async-start(), calls=%async_computation.2 | async-start | bytes 1966080
  32.0 3.8 %copy-start.7 = (f32[3,3,128]{2,1,0:T(4,128)S(1)}, f32[3,3,128]{2,1,0:T(4,128)}, u32[]{:S(2)}) copy-start(f32[3,3,128]{2,1,0:T(4,128)} %param.14) | copy-start | bytes 13828
  34.4 1.4 copy-start.5
  34.5 15.8 %collective-permute-start.1 = (bf16[4,2,3,128]{3,1,2,0:T(2,128)(2,1)S(1)}, bf16[4,2,3,128]{3,1,2,0:T(2,128)(2,1)S(1)}, u32[]{:S(2)}, u32[]{:S(2)}) collective-permute-start(bf16[4,2,3,128]{3,1,2,0:T(2,128)(2,1)S(1)} %slice.56), channel_id=1, source_target_pairs={{0,4},{4,8},{8,12},{1,5},{5,9},{9,13},{2,6},{6,10},{10,14},{3,7},{... | collective-permute-start | bytes 18440 | tf_op jit(solution)/shard_map/ppermute | solution.py:10
  52.4 1.4 copy-start.1
  52.4 4.4 %copy-start.2 = (bf16[4,384,767]{2,1,0:T(8,128)(2,1)S(1)}, bf16[4,384,767]{2,1,0:T(8,128)(2,1)}, u32[]{:S(2)}) copy-start(bf16[4,384,767]{2,1,0:T(8,128)(2,1)} %reshape.40) | copy-start | bytes 7068676
  53.9 4.4 %copy-start.3 = (bf16[4,384,1,128]{3,1,2,0:T(8,128)(2,1)}, bf16[4,384,1,128]{3,1,2,0:T(8,128)(2,1)S(1)}, u32[]{:S(2)}) copy-start(bf16[4,384,1,128]{3,1,2,0:T(8,128)(2,1)S(1)} %fusion.15) | copy-start | bytes 1179652
  58.3 13.2 %collective-permute-start = (bf16[4,384,128]{1,2,0:T(8,128)(2,1)}, bf16[4,384,128]{1,2,0:T(8,128)(2,1)S(1)}, u32[]{:S(2)}, u32[]{:S(2)}) collective-permute-start(bf16[4,384,128]{1,2,0:T(8,128)(2,1)} %get-tuple-element.183), channel_id=1, source_target_pairs={{0,4},{4,8},{8,12},{1,5},{5,9},{9,13},{2,6},{6,10},{10,14},{3,7},{... | collective-permute-start | bytes 1179656 | tf_op jit(solution)/shard_map/while/body/eval_jaxpr/ppermute | solution.py:10
  91.4 11.6 %collective-permute-start = (bf16[4,384,128]{1,2,0:T(8,128)(2,1)}, bf16[4,384,128]{1,2,0:T(8,128)(2,1)S(1)}, u32[]{:S(2)}, u32[]{:S(2)}) collective-permute-start(bf16[4,384,128]{1,2,0:T(8,128)(2,1)} %get-tuple-element.183), channel_id=1, source_target_pairs={{0,4},{4,8},{8,12},{1,5},{5,9},{9,13},{2,6},{6,10},{10,14},{3,7},{... | collective-permute-start | bytes 1179656 | tf_op jit(solution)/shard_map/while/body/eval_jaxpr/ppermute | solution.py:10
  123.0 10.7 %collective-permute-start = (bf16[4,384,128]{1,2,0:T(8,128)(2,1)}, bf16[4,384,128]{1,2,0:T(8,128)(2,1)S(1)}, u32[]{:S(2)}, u32[]{:S(2)}) collective-permute-start(bf16[4,384,128]{1,2,0:T(8,128)(2,1)} %get-tuple-element.183), channel_id=1, source_target_pairs={{0,4},{4,8},{8,12},{1,5},{5,9},{9,13},{2,6},{6,10},{10,14},{3,7},{... | collective-permute-start | bytes 1179656 | tf_op jit(solution)/shard_map/while/body/eval_jaxpr/ppermute | solution.py:10
  153.7 2.4 %copy-start.4 = (bf16[4,384,1,128]{3,1,2,0:T(8,128)(2,1)S(1)}, bf16[4,384,1,128]{3,1,2,0:T(8,128)(2,1)}, u32[]{:S(2)}) copy-start(bf16[4,384,1,128]{3,1,2,0:T(8,128)(2,1)} %copy-done.3) | copy-start | bytes 1179652
  153.7 2.4 %copy-start.6 = (bf16[128,512]{1,0:T(8,128)(2,1)S(1)}, bf16[128,512]{1,0:T(8,128)(2,1)}, u32[]{:S(2)}) copy-start(bf16[128,512]{1,0:T(8,128)(2,1)} %param.17) | copy-start | bytes 393220
  153.7 2.4 %copy-start.8 = (f32[128]{0:T(128)S(1)}, f32[128]{0:T(128)}, u32[]{:S(2)}) copy-start(f32[128]{0:T(128)} %param.16) | copy-start | bytes 1540
Sparse Core Ops, SparseCore 0:
  8.9 21.1 all-gather.1
  161.1 30.4 reduce-scatter.3
where the time goes:
time: 203 us; the launch traced here: 201 us
  waiting for transfers between devices  74.7 us (37%)
  local copies, waits for them, and re-layouts  74.3 us (37%)
  between operations  13.6 us (7%)
  other arithmetic  11.3 us (6%)
  matrix products  11.1 us (5%)
  blocking collectives  10.2 us (5%)
  starting transfers between devices  5.17 us (3%)
    ppermute x4, waiting for transfers between devices, from_behind(): return lax.ppermute(block, axis, route)  31.7 us
    unnamed x3, waiting for transfers between devices  31.3 us
    reshape x4, local copies, waits for them, and re-layouts, block_terms(): toeplitz.reshape(filter_count, block_len, 2 * block_len - 1)  25.9 us
    cond x15, local copies, waits for them, and re-layouts  17.7 us
    unnamed x29, local copies, waits for them, and re-layouts  12.2 us
    all_gather x1, waiting for transfers between devices, body(): gathered = lax.all_gather(records, 'chan', axis=2, tiled=True)  11.8 us
    slice x4, local copies, waits for them, and re-layouts, block_terms(): tiled_taps[:, block_len - 1:block_len - 1 + block_len * (2 * block_len - 1)]  11.1 us
    all_gather x1, blocking collectives, body(): all_taps = lax.all_gather(long_filter, 'seq', axis=1, tiled=True)  10.2 us
  transfers between devices with their start and end apart: 6, of which 5 were waited for; matrix products, arithmetic and copies ran while one was open for 8% of the time, Pallas kernels for 0%

commit v1 on v0

--- a/solution.py
+++ b/solution.py
@@ -1,6 +1,10 @@
+import functools
+
 import jax
 import jax.numpy as jnp
 from jax import lax
+from jax.experimental import pallas as pl
+from jax.experimental.pallas import tpu as pltpu
 from jax.sharding import PartitionSpec as P
 
 
@@ -76,6 +80,245 @@
     )
 
 
+MESH = pl.DeviceIdType.MESH
+
+
+def layer_kernel(
+    n_seq, n_chan, recs_ref, gain_ref, w_in_ref, short_ref, taps_ref, skip_ref, w_out_ref, out_ref,
+    first, second, proj, taps, strips, source, queries, gated, w_out, out_blocks,
+    z_send, z_recv, x_send, x_recv, k_send, k_recv, l_send, l_recv,
+    f_send, f_recv, w_send, w_recv, here_sem, out_sem,
+):
+    block_len, width = recs_ref.shape[1], recs_ref.shape[2]
+    length = n_seq * block_len
+    filters = taps_ref.shape[0]
+    group = width // filters
+    z = lax.axis_index("seq")
+    c = lax.axis_index("chan")
+    core_mate = (c // 2) * 2 + 1 - c % 2
+    chip_mate = (c + n_chan // 2) % n_chan
+
+    barrier = pltpu.get_barrier_semaphore()
+    for d in range(1, n_seq):
+        pl.semaphore_signal(barrier, inc=1, device_id={"seq": (z + d) % n_seq}, device_id_type=MESH)
+    for d in range(1, n_chan):
+        pl.semaphore_signal(barrier, inc=1, device_id={"chan": (c + d) % n_chan}, device_id_type=MESH)
+    pl.semaphore_wait(barrier, n_seq + n_chan - 2)
+
+    def remote(src, dst, send, recv, **device):
+        return pltpu.make_async_remote_copy(
+            src_ref=src, dst_ref=dst, send_sem=send, recv_sem=recv, device_id=device, device_id_type=MESH
+        )
+
+    def z_copy(phase, src, d):
+        held = (first, second)[phase]
+        return remote(src, held.at[z, c], z_send.at[phase, d], z_recv.at[phase, d], seq=(z + d) % n_seq)
+
+    def slot(d):
+        return (z + n_seq - d) % n_seq
+
+    def x_copy(phase, d):
+        held = (first, second)[phase]
+        block = held.at[slot(d), c]
+        return remote(block, block, x_send.at[phase, d], x_recv.at[phase, d], chan=chip_mate)
+
+    def k_copy(phase, d):
+        held = (first, second)[phase]
+        block = held.at[slot(d), c]
+        return remote(block, block, k_send.at[phase, d], k_recv.at[phase, d], chan=core_mate)
+
+    def l_copy(phase, d):
+        held = (first, second)[phase]
+        block = held.at[slot(d), chip_mate]
+        return remote(block, block, l_send.at[phase, d], l_recv.at[phase, d], chan=core_mate)
+
+    def f_copy(d):
+        return remote(taps_ref, taps.at[z], f_send.at[d], f_recv.at[d], seq=(z + d) % n_seq)
+
+    def w_copy(d):
+        there = (c + d) % n_chan
+        columns = pl.ds(pl.multiple_of(there * width, width), width)
+        rows = pl.ds(pl.multiple_of(c * width, width), width)
+        return remote(w_out_ref.at[:, columns], w_out.at[rows], w_send.at[d], w_recv.at[d], chan=there)
+
+    own_block = pltpu.make_async_copy(recs_ref.at[z], first.at[z, c], here_sem.at[0])
+    own_block.start()
+    own_taps = pltpu.make_async_copy(taps_ref, taps.at[z], here_sem.at[1])
+    own_taps.start()
+    mine = pl.ds(pl.multiple_of(c * width, width), width)
+    own_w = pltpu.make_async_copy(w_out_ref.at[:, mine], w_out.at[mine], here_sem.at[2])
+    own_w.start()
+    for d in range(1, n_seq):
+        f_copy(d).start()
+    for d in range(1, n_seq):
+        z_copy(0, recs_ref.at[(z + d) % n_seq], d).start()
+    own_block.wait()
+    x_copy(0, 0).start()
+    k_copy(0, 0).start()
+    for d in range(1, n_chan):
+        w_copy(d).start()
+
+    def build_strips():
+        own_taps.wait()
+        for d in range(1, n_seq):
+            f_copy(d).wait_recv()
+        rows = lax.broadcasted_iota(jnp.int32, (width, width), 0)
+        columns = lax.broadcasted_iota(jnp.int32, (width, width), 1)
+        mirror = jnp.where(rows + columns == width - 1, 1.0, 0.0).astype(jnp.bfloat16)
+        pieces = []
+        for s in reversed(range(n_seq)):
+            held = taps[s]
+            for j in reversed(range(block_len // width)):
+                pieces.append(
+                    jnp.dot(held[:, j * width : (j + 1) * width], mirror, preferred_element_type=jnp.float32)
+                )
+        pieces.append(jnp.zeros((filters, width), jnp.float32))
+        backward = jnp.concatenate(pieces, axis=1)
+        for f in range(filters):
+            row = jnp.broadcast_to(backward[f : f + 1], (width, length + width))
+            turned = pltpu.roll(row, 1, 1, stride=1, stride_axis=0)
+            strips[f * width : (f + 1) * width, :] = turned[:, width:].astype(jnp.bfloat16)
+
+    gain = gain_ref[...]
+
+    def project(d):
+        s = slot(d)
+        wide = jnp.concatenate([first[s, j] for j in range(n_chan)], axis=1).astype(jnp.float32)
+        inv_rms = lax.rsqrt(jnp.mean(wide * wide, axis=-1, keepdims=True) + 1e-06)
+        normed = (wide * inv_rms * gain).astype(jnp.bfloat16)
+        got = jnp.dot(normed, w_in_ref[...], preferred_element_type=jnp.float32)
+        rows = pl.ds(pl.multiple_of(8 + s * block_len, 8), block_len)
+        proj[rows, :] = got.astype(jnp.bfloat16).astype(jnp.float32)
+
+    def gather_block(phase, d):
+        if d > 0:
+            z_copy(phase, first.at[0, 0], d).wait_recv()
+            x_copy(phase, d).start()
+            k_copy(phase, d).start()
+
+    def relay_block(phase, d):
+        x_copy(phase, d).wait_recv()
+        l_copy(phase, d).start()
+
+    def finish_block(phase, d):
+        k_copy(phase, d).wait_recv()
+        l_copy(phase, d).wait_recv()
+
+    proj[0:8, :] = jnp.zeros((8, proj.shape[1]), jnp.float32)
+    for d in range(n_seq):
+        if d + 1 < n_seq:
+            gather_block(0, d + 1)
+        relay_block(0, d)
+        if d == 0:
+            build_strips()
+        finish_block(0, d)
+        project(d)
+
+    short = short_ref[...]
+    skip = skip_ref[...]
+    lane_group = lax.broadcasted_iota(jnp.int32, (width, width), 1) // group
+    per_block = block_len // width
+    for i in range(length // width):
+        now = proj[8 + i * width : 8 + (i + 1) * width, :]
+        back1 = proj[7 + i * width : 7 + (i + 1) * width, :]
+        back2 = proj[6 + i * width : 6 + (i + 1) * width, :]
+        streams = short[0:1] * now + short[1:2] * back1 + short[2:3] * back2
+        query = streams[:, 0:width]
+        src = (streams[:, width : 2 * width] * streams[:, 2 * width :]).astype(jnp.bfloat16)
+        source[i * width : (i + 1) * width, :] = src
+        depth = (i + 1) * width
+        sums = jnp.dot(strips[:, length - depth :], source[0:depth, :], preferred_element_type=jnp.float32)
+        total = sums[0:width]
+        for f in range(1, filters):
+            total = jnp.where(lane_group == f, sums[f * width : (f + 1) * width], total)
+        total = total + skip * src.astype(jnp.float32)
+        b, part = divmod(i, per_block)
+        gated[b, part * width : (part + 1) * width, :] = (query * total).astype(jnp.bfloat16)
+        if part == per_block - 1:
+
+            @pl.when(b == z)
+            def _():
+                keep = pltpu.make_async_copy(gated.at[b], second.at[z, c], here_sem.at[3])
+                keep.start()
+                keep.wait()
+                x_copy(1, 0).start()
+                k_copy(1, 0).start()
+
+            @pl.when(b != z)
+            def _():
+                z_copy(1, gated.at[b], (b + n_seq - z) % n_seq).start()
+
+    own_w.wait()
+    for d in range(1, n_chan):
+        w_copy(d).wait_recv()
+    for d in range(n_seq):
+        if d + 1 < n_seq:
+            gather_block(1, d + 1)
+        relay_block(1, d)
+        finish_block(1, d)
+        s = slot(d)
+        wide = jnp.concatenate([second[s, j] for j in range(n_chan)], axis=1)
+        got = jnp.dot(wide, w_out[...], preferred_element_type=jnp.float32)
+        out_blocks[s] = got.astype(jnp.bfloat16)
+        pltpu.make_async_copy(out_blocks.at[s], out_ref.at[s], out_sem.at[d]).start()
+
+    for phase in range(2):
+        for d in range(n_seq):
+            if d > 0:
+                z_copy(phase, first.at[0, 0], d).wait_send()
+            x_copy(phase, d).wait_send()
+            k_copy(phase, d).wait_send()
+            l_copy(phase, d).wait_send()
+    for d in range(1, n_seq):
+        f_copy(d).wait_send()
+    for d in range(1, n_chan):
+        w_copy(d).wait_send()
+    for d in range(n_seq):
+        pltpu.make_async_copy(out_blocks.at[slot(d)], out_ref.at[slot(d)], out_sem.at[d]).wait()
+
+
+def by_record(n_seq, n_chan, records, norm_gain, in_projection, short_kernel, long_filter, skip_gain, out_projection):
+    record_count, block_len, width = records.shape
+    length = n_seq * block_len
+    filters = long_filter.shape[0]
+    vmem = pl.BlockSpec(memory_space=pltpu.VMEM)
+    anywhere = pl.BlockSpec(memory_space=pl.ANY)
+    dma = pltpu.SemaphoreType.DMA
+    return pl.pallas_call(
+        functools.partial(layer_kernel, n_seq, n_chan),
+        out_shape=jax.ShapeDtypeStruct(records.shape, jnp.bfloat16),
+        in_specs=[anywhere, vmem, vmem, vmem, anywhere, vmem, anywhere],
+        out_specs=anywhere,
+        scratch_shapes=[
+            pltpu.VMEM((n_seq, n_chan, block_len, width), jnp.bfloat16),
+            pltpu.VMEM((n_seq, n_chan, block_len, width), jnp.bfloat16),
+            pltpu.VMEM((8 + length, 3 * width), jnp.float32),
+            pltpu.VMEM((n_seq, filters, block_len), jnp.bfloat16),
+            pltpu.VMEM((filters * width, length), jnp.bfloat16),
+            pltpu.VMEM((length, width), jnp.bfloat16),
+            pltpu.VMEM((8, width), jnp.float32),
+            pltpu.VMEM((n_seq, block_len, width), jnp.bfloat16),
+            pltpu.VMEM((n_chan * width, width), jnp.bfloat16),
+            pltpu.VMEM((record_count, block_len, width), jnp.bfloat16),
+        ]
+        + [dma((2, n_seq))] * 8
+        + [dma((n_seq,))] * 2
+        + [dma((n_chan,))] * 2
+        + [dma((4,)), dma((n_seq,))],
+        compiler_params=pltpu.CompilerParams(
+            collective_id=0, has_side_effects=True, vmem_limit_bytes=48 * 1024 * 1024
+        ),
+    )(
+        records,
+        norm_gain[None, :],
+        in_projection.reshape(in_projection.shape[0], -1),
+        short_kernel.reshape(3, -1),
+        long_filter,
+        skip_gain[None, :],
+        out_projection,
+    )
+
+
 def solution(mesh):
     placed = (
         P("parts", "seq", "chan"),
@@ -86,6 +329,18 @@
         P("chan"),
         P("chan", None),
     )
-    return jax.shard_map(
-        body, mesh=mesh, in_specs=placed, out_specs=P("parts", "seq", "chan"), check_vma=False
-    )
+    n_seq, n_chan, n_parts = mesh.shape["seq"], mesh.shape["chan"], mesh.shape["parts"]
+
+    def apply(*args):
+        records = args[0]
+        block_len, width = records.shape[1] // n_seq, records.shape[2] // n_chan
+        whole_records = records.shape[0] // n_parts == n_seq
+        if whole_records and n_chan == 4 and width == 128 and block_len % width == 0:
+            chosen = functools.partial(by_record, n_seq, n_chan)
+        else:
+            chosen = body
+        return jax.shard_map(
+            chosen, mesh=mesh, in_specs=placed, out_specs=P("parts", "seq", "chan"), check_vma=False
+        )(*args)
+
+    return apply

time: 203 us -> 48.6 us (0.24); the launches traced: 201 us -> 48.4 us
  waiting for transfers between devices: 74.7 us -> 0 us
  local copies, waits for them, and re-layouts: 74.3 us -> 3.59 us
  Pallas kernels: 0 us -> 44.8 us
  between operations: 13.6 us -> 0.07 us
  other arithmetic: 11.3 us -> 0 us
  matrix products: 11.1 us -> 0 us
  blocking collectives: 10.2 us -> 0 us
  starting transfers between devices: 5.17 us -> 0 us
    pallas_call x0 -> x1, Pallas kernels: none -> 44.8 us  [by_record(): pl.pallas_call(functools.partial(layer_kernel, n_seq, n_chan), out_shape=...]
    ppermute x4 -> x0, waiting for transfers between devices: 31.7 us -> none  [from_behind(): return lax.ppermute(block, axis, route)]
    unnamed x3 -> x0, waiting for transfers between devices: 31.3 us -> none
    reshape x8 -> x1, local copies, waits for them, and re-layouts: 27.2 us -> 0.21 us  [by_record(): in_projection.reshape(in_projection.shape[0], -1)]
    cond x15 -> x0, local copies, waits for them, and re-layouts: 17.7 us -> none
    all_gather x1 -> x0, waiting for transfers between devices: 11.8 us -> none  [body(): gathered = lax.all_gather(records, 'chan', axis=2, tiled=True)]
    slice x5 -> x0, local copies, waits for them, and re-layouts: 11.1 us -> none  [the longest x4 11.1 us: block_terms(): tiled_taps[:, block_len - 1:block_len - 1 + block_len * (2 * block_len - 1)]]
    all_gather x1 -> x0, blocking collectives: 10.2 us -> none  [body(): all_taps = lax.all_gather(long_filter, 'seq', axis=1, tiled=True)]
  transfers between devices with their start and end apart: 6 -> 0, of which waited for: 5 -> 0; matrix products, arithmetic and copies ran while one was open for 8% -> 0% of each run, Pallas kernels for 0% -> 0%
where the time goes in v1:
time: 48.6 us; the launch traced here: 48.4 us
  Pallas kernels  44.8 us (92%)
  local copies, waits for them, and re-layouts  3.59 us (7%)
    pallas_call x1, Pallas kernels, by_record(): pl.pallas_call(functools.partial(layer_kernel, n_seq, n_chan), out_shape=...  44.8 us
    unnamed x13, local copies, waits for them, and re-layouts  3.38 us

profile of v1, /device:TPU:29, one launch (start us, length us, event | category | flops | bytes accessed | tf_op | source)
XLA Modules:
  0.0 48.4 jit_solution(14746494932289909621)
XLA Ops:
  0.0 0.7 %copy.13 = f32[1,3,3,128]{3,1,2,0:T(4,128)S(1)} copy(f32[1,3,3,128]{3,2,1,0:T(4,128)} %bitcast.11) | data formatting | bytes 9216
  0.7 1.2 %copy.9 = bf16[512,3,128]{0,2,1:T(8,128)(2,1)S(1)} copy(bf16[512,3,128]{2,0,1:T(8,128)(2,1)} %param.9) | data formatting | bytes 786432 | tf_op args[2]
  1.9 0.0 copy-start
  1.9 0.0 copy-start.1
  1.9 0.0 copy-start.2
  1.9 0.0 copy-start.3
  1.9 0.0 copy-start.4
  1.9 0.2 copy.10.w_in_ref
  2.1 0.7 %copy-done = bf16[4,384,128]{2,1,0:T(8,128)(2,1)S(1)} copy-done((bf16[4,384,128]{2,1,0:T(8,128)(2,1)S(1)}, bf16[4,384,128]{2,1,0:T(8,128)(2,1)}, u32[]{:S(2)}) %copy-start) | copy-done | bytes 393240
  2.9 0.0 copy-done.1
  2.9 0.0 copy-done.2
  2.9 0.0 copy-done.3
  2.9 0.0 copy-done.4
  2.9 44.8 %shard_map.73 = bf16[4,384,128]{2,1,0:T(8,128)(2,1)S(1)} custom-call(bf16[4,384,128]{2,1,0:T(8,128)(2,1)S(1)} %copy-done, f32[1,512]{1,0:T(1,128)S(1)} %bitcast.8, bf16[512,384]{1,0:T(8,128)(2,1)S(1)} %copy.10.w_in_ref, f32[3,384]{1,0:T(4,128)S(1)} %bitcast.7, bf16[4,384]{1,0:T(4,128)(2,1)S(1)} %copy-done.2, f32[1,128]{1,0:T(1,128)S(1)} %bitcast.9, ...), custom_call_target="tpu_custom_call" | custom-call | tf_op jit(solution)/shard_map/pallas_call | solution.py:287
  47.7 0.7 %copy.15 = bf16[4,384,128]{2,1,0:T(8,128)(2,1)} copy(bf16[4,384,128]{2,1,0:T(8,128)(2,1)S(1)} %shard_map.73) | data formatting | bytes 786432
Async XLA Ops:
  1.9 1.0 %copy-start = (bf16[4,384,128]{2,1,0:T(8,128)(2,1)S(1)}, bf16[4,384,128]{2,1,0:T(8,128)(2,1)}, u32[]{:S(2)}) copy-start(bf16[4,384,128]{2,1,0:T(8,128)(2,1)} %recs_ref.1) | copy-start | bytes 1179652
  1.9 1.0 %copy-start.1 = (bf16[128,512]{1,0:T(8,128)(2,1)S(1)}, bf16[128,512]{1,0:T(8,128)(2,1)}, u32[]{:S(2)}) copy-start(bf16[128,512]{1,0:T(8,128)(2,1)} %w_out_ref.1) | copy-start | bytes 393220
  1.9 1.0 %copy-start.2 = (bf16[4,384]{1,0:T(4,128)(2,1)S(1)}, bf16[4,384]{1,0:T(4,128)(2,1)}, u32[]{:S(2)}) copy-start(bf16[4,384]{1,0:T(4,128)(2,1)} %taps_ref.1) | copy-start | bytes 9220
  1.9 1.0 %copy-start.3 = (f32[512]{0:T(512)S(1)}, f32[512]{0:T(512)}, u32[]{:S(2)}) copy-start(f32[512]{0:T(512)} %param.8) | copy-start | bytes 6148
  1.9 1.0 %copy-start.4 = (f32[128]{0:T(128)S(1)}, f32[128]{0:T(128)}, u32[]{:S(2)}) copy-start(f32[128]{0:T(128)} %param.12) | copy-start | bytes 1540

commit v2 on v1

--- a/solution.py
+++ b/solution.py
@@ -84,8 +84,8 @@
 
 
 def layer_kernel(
-    n_seq, n_chan, recs_ref, gain_ref, w_in_ref, short_ref, taps_ref, skip_ref, w_out_ref, out_ref,
-    first, second, proj, taps, strips, source, queries, gated, w_out, out_blocks,
+    n_seq, n_chan, recs_ref, gain_hbm, w_in_hbm, short_hbm, taps_ref, skip_hbm, w_out_ref, out_ref,
+    gain_ref, w_in_ref, short_ref, skip_ref, out_blocks, first, second, proj, taps, strips, source, gated, w_out,
     z_send, z_recv, x_send, x_recv, k_send, k_recv, l_send, l_recv,
     f_send, f_recv, w_send, w_recv, here_sem, out_sem,
 ):
@@ -110,27 +110,46 @@
             src_ref=src, dst_ref=dst, send_sem=send, recv_sem=recv, device_id=device, device_id_type=MESH
         )
 
-    def z_copy(phase, src, d):
-        held = (first, second)[phase]
-        return remote(src, held.at[z, c], z_send.at[phase, d], z_recv.at[phase, d], seq=(z + d) % n_seq)
-
-    def slot(d):
-        return (z + n_seq - d) % n_seq
-
-    def x_copy(phase, d):
-        held = (first, second)[phase]
-        block = held.at[slot(d), c]
-        return remote(block, block, x_send.at[phase, d], x_recv.at[phase, d], chan=chip_mate)
-
-    def k_copy(phase, d):
-        held = (first, second)[phase]
-        block = held.at[slot(d), c]
-        return remote(block, block, k_send.at[phase, d], k_recv.at[phase, d], chan=core_mate)
-
-    def l_copy(phase, d):
-        held = (first, second)[phase]
-        block = held.at[slot(d), chip_mate]
-        return remote(block, block, l_send.at[phase, d], l_recv.at[phase, d], chan=core_mate)
+    held = (first, second)
+
+    def give(phase, src, there):
+        return remote(src, held[phase].at[z, c], z_send.at[phase, there], z_recv.at[phase, z], seq=there)
+
+    def given(phase, s):
+        block = held[phase].at[s, c]
+        return remote(block, block, z_send.at[phase, s], z_recv.at[phase, s], seq=s)
+
+    def x_copy(phase, s, src=None):
+        block = held[phase].at[s, c]
+        src = block if src is None else src
+        return remote(src, block, x_send.at[phase, s], x_recv.at[phase, s], chan=chip_mate)
+
+    def k_copy(phase, s, src=None):
+        block = held[phase].at[s, c]
+        src = block if src is None else src
+        return remote(src, block, k_send.at[phase, s], k_recv.at[phase, s], chan=core_mate)
+
+    def l_copy(phase, s):
+        block = held[phase].at[s, chip_mate]
+        return remote(block, block, l_send.at[phase, s], l_recv.at[phase, s], chan=core_mate)
+
+    def spread(phase, s):
+        given(phase, s).wait_recv()
+        x_copy(phase, s).start()
+        k_copy(phase, s).start()
+
+    def relay(phase, s):
+        x_copy(phase, s).wait_recv()
+        l_copy(phase, s).start()
+
+    def finish(phase, s):
+        k_copy(phase, s).wait_recv()
+        l_copy(phase, s).wait_recv()
+
+    def others(s, act):
+        @pl.when(s != z)
+        def _():
+            act(0, s)
 
     def f_copy(d):
         return remote(taps_ref, taps.at[z], f_send.at[d], f_recv.at[d], seq=(z + d) % n_seq)
@@ -141,6 +160,21 @@
         rows = pl.ds(pl.multiple_of(c * width, width), width)
         return remote(w_out_ref.at[:, columns], w_out.at[rows], w_send.at[d], w_recv.at[d], chan=there)
 
+    x_copy(0, z, recs_ref.at[z]).start()
+    for d in range(1, n_seq):
+        f_copy(d).start()
+    for j in range(1, n_seq):
+        ahead, back = n_seq - j, n_seq - 1 - j
+
+        @pl.when(ahead > z)
+        def _():
+            give(0, recs_ref.at[ahead], ahead).start()
+
+        @pl.when(back < z)
+        def _():
+            give(0, recs_ref.at[back], back).start()
+
+    k_copy(0, z, recs_ref.at[z]).start()
     own_block = pltpu.make_async_copy(recs_ref.at[z], first.at[z, c], here_sem.at[0])
     own_block.start()
     own_taps = pltpu.make_async_copy(taps_ref, taps.at[z], here_sem.at[1])
@@ -148,15 +182,16 @@
     mine = pl.ds(pl.multiple_of(c * width, width), width)
     own_w = pltpu.make_async_copy(w_out_ref.at[:, mine], w_out.at[mine], here_sem.at[2])
     own_w.start()
-    for d in range(1, n_seq):
-        f_copy(d).start()
-    for d in range(1, n_seq):
-        z_copy(0, recs_ref.at[(z + d) % n_seq], d).start()
-    own_block.wait()
-    x_copy(0, 0).start()
-    k_copy(0, 0).start()
     for d in range(1, n_chan):
         w_copy(d).start()
+    fetched = [
+        pltpu.make_async_copy(src, dst, here_sem.at[4 + j])
+        for j, (src, dst) in enumerate(
+            [(gain_hbm, gain_ref), (w_in_hbm, w_in_ref), (short_hbm, short_ref), (skip_hbm, skip_ref)]
+        )
+    ]
+    for copy in fetched:
+        copy.start()
 
     def build_strips():
         own_taps.wait()
@@ -179,50 +214,28 @@
             turned = pltpu.roll(row, 1, 1, stride=1, stride_axis=0)
             strips[f * width : (f + 1) * width, :] = turned[:, width:].astype(jnp.bfloat16)
 
+    for copy in fetched:
+        copy.wait()
     gain = gain_ref[...]
 
-    def project(d):
-        s = slot(d)
+    def project(s):
         wide = jnp.concatenate([first[s, j] for j in range(n_chan)], axis=1).astype(jnp.float32)
         inv_rms = lax.rsqrt(jnp.mean(wide * wide, axis=-1, keepdims=True) + 1e-06)
         normed = (wide * inv_rms * gain).astype(jnp.bfloat16)
-        got = jnp.dot(normed, w_in_ref[...], preferred_element_type=jnp.float32)
-        rows = pl.ds(pl.multiple_of(8 + s * block_len, 8), block_len)
-        proj[rows, :] = got.astype(jnp.bfloat16).astype(jnp.float32)
-
-    def gather_block(phase, d):
-        if d > 0:
-            z_copy(phase, first.at[0, 0], d).wait_recv()
-            x_copy(phase, d).start()
-            k_copy(phase, d).start()
-
-    def relay_block(phase, d):
-        x_copy(phase, d).wait_recv()
-        l_copy(phase, d).start()
-
-    def finish_block(phase, d):
-        k_copy(phase, d).wait_recv()
-        l_copy(phase, d).wait_recv()
-
-    proj[0:8, :] = jnp.zeros((8, proj.shape[1]), jnp.float32)
-    for d in range(n_seq):
-        if d + 1 < n_seq:
-            gather_block(0, d + 1)
-        relay_block(0, d)
-        if d == 0:
-            build_strips()
-        finish_block(0, d)
-        project(d)
-
-    short = short_ref[...]
+        weights = jnp.concatenate([w_in_ref[k] for k in range(3)], axis=1)
+        got = jnp.dot(normed, weights, preferred_element_type=jnp.float32)
+        proj[8 + s * block_len : 8 + (s + 1) * block_len, :] = got.astype(jnp.bfloat16).astype(jnp.float32)
+
+    short = [jnp.concatenate([short_ref[j, k : k + 1] for k in range(3)], axis=1) for j in range(3)]
     skip = skip_ref[...]
     lane_group = lax.broadcasted_iota(jnp.int32, (width, width), 1) // group
     per_block = block_len // width
-    for i in range(length // width):
+
+    def convolve(i):
         now = proj[8 + i * width : 8 + (i + 1) * width, :]
         back1 = proj[7 + i * width : 7 + (i + 1) * width, :]
         back2 = proj[6 + i * width : 6 + (i + 1) * width, :]
-        streams = short[0:1] * now + short[1:2] * back1 + short[2:3] * back2
+        streams = short[0] * now + short[1] * back1 + short[2] * back2
         query = streams[:, 0:width]
         src = (streams[:, width : 2 * width] * streams[:, 2 * width :]).astype(jnp.bfloat16)
         source[i * width : (i + 1) * width, :] = src
@@ -234,85 +247,118 @@
         total = total + skip * src.astype(jnp.float32)
         b, part = divmod(i, per_block)
         gated[b, part * width : (part + 1) * width, :] = (query * total).astype(jnp.bfloat16)
-        if part == per_block - 1:
-
-            @pl.when(b == z)
+
+    def send_gated(b):
+        @pl.when(b == z)
+        def _():
+            x_copy(1, z, gated.at[b]).start()
+            k_copy(1, z, gated.at[b]).start()
+            pltpu.make_async_copy(gated.at[b], second.at[z, c], here_sem.at[3]).start()
+
+        @pl.when(b != z)
+        def _():
+            give(1, gated.at[b], b).start()
+
+    def behind(e):
+        return (z + n_seq - e) % n_seq
+
+    proj[0:8, :] = jnp.zeros((8, proj.shape[1]), jnp.float32)
+    build_strips()
+    others(0, spread)
+    relay(0, z)
+    own_block.wait()
+    for b in range(n_seq):
+        if b + 1 < n_seq:
+            others(b + 1, spread)
+        others(b, relay)
+        finish(0, b)
+        project(b)
+        for part in range(per_block):
+            convolve(b * per_block + part)
+        send_gated(b)
+        for e in range(1, b + 1):
+
+            @pl.when(b - z == e)
             def _():
-                keep = pltpu.make_async_copy(gated.at[b], second.at[z, c], here_sem.at[3])
-                keep.start()
-                keep.wait()
-                x_copy(1, 0).start()
-                k_copy(1, 0).start()
-
-            @pl.when(b != z)
-            def _():
-                z_copy(1, gated.at[b], (b + n_seq - z) % n_seq).start()
+                spread(1, behind(e))
+                relay(1, behind(e - 1))
 
     own_w.wait()
     for d in range(1, n_chan):
         w_copy(d).wait_recv()
-    for d in range(n_seq):
-        if d + 1 < n_seq:
-            gather_block(1, d + 1)
-        relay_block(1, d)
-        finish_block(1, d)
-        s = slot(d)
+    for e in range(1, n_seq):
+
+        @pl.when(e > n_seq - 1 - z)
+        def _():
+            spread(1, behind(e))
+            relay(1, behind(e - 1))
+
+    relay(1, behind(n_seq - 1))
+    pltpu.make_async_copy(gated.at[0], second.at[z, c], here_sem.at[3]).wait()
+    for e in range(n_seq):
+        s = behind(e)
+        finish(1, s)
         wide = jnp.concatenate([second[s, j] for j in range(n_chan)], axis=1)
         got = jnp.dot(wide, w_out[...], preferred_element_type=jnp.float32)
         out_blocks[s] = got.astype(jnp.bfloat16)
-        pltpu.make_async_copy(out_blocks.at[s], out_ref.at[s], out_sem.at[d]).start()
+        pltpu.make_async_copy(out_blocks.at[s], out_ref.at[s], out_sem.at[e]).start()
 
     for phase in range(2):
-        for d in range(n_seq):
-            if d > 0:
-                z_copy(phase, first.at[0, 0], d).wait_send()
-            x_copy(phase, d).wait_send()
-            k_copy(phase, d).wait_send()
-            l_copy(phase, d).wait_send()
+        for s in range(n_seq):
+
+            @pl.when(s != z)
+            def _():
+                given(phase, s).wait_send()
+
+            x_copy(phase, s).wait_send()
+            k_copy(phase, s).wait_send()
+            l_copy(phase, s).wait_send()
     for d in range(1, n_seq):
         f_copy(d).wait_send()
     for d in range(1, n_chan):
         w_copy(d).wait_send()
-    for d in range(n_seq):
-        pltpu.make_async_copy(out_blocks.at[slot(d)], out_ref.at[slot(d)], out_sem.at[d]).wait()
+    for e in range(n_seq):
+        pltpu.make_async_copy(out_blocks.at[behind(e)], out_ref.at[behind(e)], out_sem.at[e]).wait()
 
 
 def by_record(n_seq, n_chan, records, norm_gain, in_projection, short_kernel, long_filter, skip_gain, out_projection):
-    record_count, block_len, width = records.shape
+    _, block_len, width = records.shape
     length = n_seq * block_len
     filters = long_filter.shape[0]
-    vmem = pl.BlockSpec(memory_space=pltpu.VMEM)
-    anywhere = pl.BlockSpec(memory_space=pl.ANY)
+    hbm = pl.BlockSpec(memory_space=pltpu.HBM)
     dma = pltpu.SemaphoreType.DMA
     return pl.pallas_call(
         functools.partial(layer_kernel, n_seq, n_chan),
         out_shape=jax.ShapeDtypeStruct(records.shape, jnp.bfloat16),
-        in_specs=[anywhere, vmem, vmem, vmem, anywhere, vmem, anywhere],
-        out_specs=anywhere,
+        in_specs=[hbm] * 7,
+        out_specs=hbm,
         scratch_shapes=[
+            pltpu.VMEM((1, n_chan * width), jnp.float32),
+            pltpu.VMEM((3, n_chan * width, width), jnp.bfloat16),
+            pltpu.VMEM((3, 3, width), jnp.float32),
+            pltpu.VMEM((1, width), jnp.float32),
+            pltpu.VMEM(records.shape, jnp.bfloat16),
             pltpu.VMEM((n_seq, n_chan, block_len, width), jnp.bfloat16),
             pltpu.VMEM((n_seq, n_chan, block_len, width), jnp.bfloat16),
             pltpu.VMEM((8 + length, 3 * width), jnp.float32),
             pltpu.VMEM((n_seq, filters, block_len), jnp.bfloat16),
             pltpu.VMEM((filters * width, length), jnp.bfloat16),
             pltpu.VMEM((length, width), jnp.bfloat16),
-            pltpu.VMEM((8, width), jnp.float32),
             pltpu.VMEM((n_seq, block_len, width), jnp.bfloat16),
             pltpu.VMEM((n_chan * width, width), jnp.bfloat16),
-            pltpu.VMEM((record_count, block_len, width), jnp.bfloat16),
         ]
         + [dma((2, n_seq))] * 8
         + [dma((n_seq,))] * 2
         + [dma((n_chan,))] * 2
-        + [dma((4,)), dma((n_seq,))],
+        + [dma((8,)), dma((n_seq,))],
         compiler_params=pltpu.CompilerParams(
-            collective_id=0, has_side_effects=True, vmem_limit_bytes=48 * 1024 * 1024
+            collective_id=0, has_side_effects=True, vmem_limit_bytes=63 * 1024 * 1024
         ),
     )(
         records,
         norm_gain[None, :],
-        in_projection.reshape(in_projection.shape[0], -1),
-        short_kernel.reshape(3, -1),
+        in_projection.transpose(1, 0, 2),
+        short_kernel,
         long_filter,
         skip_gain[None, :],
         out_projection,

time: 48.6 us -> 44.5 us (0.916)
  Pallas kernels: 44.8 us -> 42.5 us
  local copies, waits for them, and re-layouts: 3.59 us -> 1.77 us
    pallas_call x1, Pallas kernels: 44.8 us -> 42.5 us  [by_record(): pl.pallas_call(functools.partial(layer_kernel, n_seq, n_chan), out_shape=...]
    unnamed x13 -> x1, local copies, waits for them, and re-layouts: 3.38 us -> 1.77 us
where the time goes in v2:
time: 44.5 us; the launch traced here: 44.3 us
  Pallas kernels  42.5 us (96%)
  local copies, waits for them, and re-layouts  1.77 us (4%)
    pallas_call x1, Pallas kernels, by_record(): pl.pallas_call(functools.partial(layer_kernel, n_seq, n_chan), out_shape=...  42.5 us
    unnamed x1, local copies, waits for them, and re-layouts  1.77 us

profile of v2, /device:TPU:29, one launch (start us, length us, event | category | flops | bytes accessed | tf_op | source)
XLA Modules:
  0.0 44.3 jit_solution(13547275519370771548)
XLA Ops:
  0.0 42.5 %shard_map.73 = bf16[4,384,128]{2,1,0:T(8,128)(2,1)} custom-call(bf16[4,384,128]{2,1,0:T(8,128)(2,1)} %recs_ref.1, f32[1,512]{1,0:T(1,128)} %bitcast.4, bf16[3,512,128]{2,1,0:T(8,128)(2,1)} %bitcast.3, f32[3,3,128]{2,1,0:T(4,128)} %short_hbm.1, bf16[4,384]{1,0:T(4,128)(2,1)} %taps_ref.1, f32[1,128]{1,0:T(1,128)} %bitcast.5, bf16[128,512]{1,0:T(8,128)(2,1)} %w_out_ref.1), custom_call_target="tpu_custom_call" | custom-call | tf_op jit(solution)/shard_map/pallas_call | solution.py:330
  42.5 1.8 %copy.9 = bf16[4,384,128]{2,1,0:T(8,128)(2,1)} copy(bf16[4,384,128]{2,1,0:T(8,128)(2,1)} %shard_map.73) | data formatting | bytes 786432

commit v3 on v2

--- a/solution.py
+++ b/solution.py
@@ -264,12 +264,11 @@
 
     proj[0:8, :] = jnp.zeros((8, proj.shape[1]), jnp.float32)
     build_strips()
-    others(0, spread)
+    for b in range(n_seq):
+        others(b, spread)
     relay(0, z)
     own_block.wait()
     for b in range(n_seq):
-        if b + 1 < n_seq:
-            others(b + 1, spread)
         others(b, relay)
         finish(0, b)
         project(b)

time: 44.5 us -> 41.6 us (0.935)
  Pallas kernels: 42.5 us -> 39.6 us
    pallas_call x1, Pallas kernels: 42.5 us -> 39.6 us  [by_record(): pl.pallas_call(functools.partial(layer_kernel, n_seq, n_chan), out_shape=...]
where the time goes in v3:
time: 41.6 us; the launch traced here: 41.4 us
  Pallas kernels  39.6 us (95%)
  local copies, waits for them, and re-layouts  1.77 us (4%)
    pallas_call x1, Pallas kernels, by_record(): pl.pallas_call(functools.partial(layer_kernel, n_seq, n_chan), out_shape=...  39.6 us
    unnamed x1, local copies, waits for them, and re-layouts  1.77 us

profile of v3, /device:TPU:29, one launch (start us, length us, event | category | flops | bytes accessed | tf_op | source)
XLA Modules:
  0.0 41.4 jit_solution(10694072075194338221)
XLA Ops:
  0.0 39.6 %shard_map.73 = bf16[4,384,128]{2,1,0:T(8,128)(2,1)} custom-call(bf16[4,384,128]{2,1,0:T(8,128)(2,1)} %recs_ref.1, f32[1,512]{1,0:T(1,128)} %bitcast.4, bf16[3,512,128]{2,1,0:T(8,128)(2,1)} %bitcast.3, f32[3,3,128]{2,1,0:T(4,128)} %short_hbm.1, bf16[4,384]{1,0:T(4,128)(2,1)} %taps_ref.1, f32[1,128]{1,0:T(1,128)} %bitcast.5, bf16[128,512]{1,0:T(8,128)(2,1)} %w_out_ref.1), custom_call_target="tpu_custom_call" | custom-call | tf_op jit(solution)/shard_map/pallas_call | solution.py:329
  39.6 1.8 %copy.9 = bf16[4,384,128]{2,1,0:T(8,128)(2,1)} copy(bf16[4,384,128]{2,1,0:T(8,128)(2,1)} %shard_map.73) | data formatting | bytes 786432

commit v4 on v3

--- a/solution.py
+++ b/solution.py
@@ -263,9 +263,10 @@
         return (z + n_seq - e) % n_seq
 
     proj[0:8, :] = jnp.zeros((8, proj.shape[1]), jnp.float32)
-    build_strips()
     for b in range(n_seq):
         others(b, spread)
+        if b == 0:
+            build_strips()
     relay(0, z)
     own_block.wait()
     for b in range(n_seq):
@@ -280,7 +281,6 @@
             @pl.when(b - z == e)
             def _():
                 spread(1, behind(e))
-                relay(1, behind(e - 1))
 
     own_w.wait()
     for d in range(1, n_chan):
@@ -290,9 +290,9 @@
         @pl.when(e > n_seq - 1 - z)
         def _():
             spread(1, behind(e))
-            relay(1, behind(e - 1))
-
-    relay(1, behind(n_seq - 1))
+
+    for e in range(n_seq):
+        relay(1, behind(e))
     pltpu.make_async_copy(gated.at[0], second.at[z, c], here_sem.at[3]).wait()
     for e in range(n_seq):
         s = behind(e)

time: 41.6 us -> 40.2 us (0.966)
  Pallas kernels: 39.6 us -> 38.2 us
    pallas_call x1, Pallas kernels: 39.6 us -> 38.2 us  [by_record(): pl.pallas_call(functools.partial(layer_kernel, n_seq, n_chan), out_shape=...]
where the time goes in v4:
time: 40.2 us; the launch traced here: 40 us
  Pallas kernels  38.2 us (95%)
  local copies, waits for them, and re-layouts  1.77 us (4%)
    pallas_call x1, Pallas kernels, by_record(): pl.pallas_call(functools.partial(layer_kernel, n_seq, n_chan), out_shape=...  38.2 us
    unnamed x1, local copies, waits for them, and re-layouts  1.77 us

profile of v4, /device:TPU:29, one launch (start us, length us, event | category | flops | bytes accessed | tf_op | source)
XLA Modules:
  0.0 40.0 jit_solution(4470478316895527365)
XLA Ops:
  0.0 38.2 %shard_map.73 = bf16[4,384,128]{2,1,0:T(8,128)(2,1)} custom-call(bf16[4,384,128]{2,1,0:T(8,128)(2,1)} %recs_ref.1, f32[1,512]{1,0:T(1,128)} %bitcast.4, bf16[3,512,128]{2,1,0:T(8,128)(2,1)} %bitcast.3, f32[3,3,128]{2,1,0:T(4,128)} %short_hbm.1, bf16[4,384]{1,0:T(4,128)(2,1)} %taps_ref.1, f32[1,128]{1,0:T(1,128)} %bitcast.5, bf16[128,512]{1,0:T(8,128)(2,1)} %w_out_ref.1), custom_call_target="tpu_custom_call" | custom-call | tf_op jit(solution)/shard_map/pallas_call | solution.py:329
  38.3 1.8 %copy.9 = bf16[4,384,128]{2,1,0:T(8,128)(2,1)} copy(bf16[4,384,128]{2,1,0:T(8,128)(2,1)} %shard_map.73) | data formatting | bytes 786432
